TPU v7x, 256 devices: a whole 4x4x8 slice. The times are simulated.
256 devices in a mesh: ctx: 16 (over x_hi, y, core), exp: 16 (over z, x_lo).
Axes of the slice: x: 4 (x_hi: 2, x_lo: 2; x = x_hi * 2 + x_lo), y: 4, z: 8, core: 2. Of those that a mesh axis runs over, the one named last changes fastest.
Arguments:
- query: bfloat16 [1024, 8192], P('ctx', 'exp'), may hold values from -7 to 7
- keys: bfloat16 [32768, 512], P('ctx'), may hold values from -9 to 9
- values: bfloat16 [32768, 512], P('ctx'), may hold values from -6 to 6
- out_weight: bfloat16 [8192, 4096], P('exp'), may hold values from -3 to 3
- residual: bfloat16 [1024, 4096], P(('ctx', 'exp')), may hold values from -6 to 6
- norm_gain: float32 [4096], replicated, may hold values from 0.1 to 1.9
- expert_ids: int32 [1024, 8], P(('ctx', 'exp')), may hold values from 0 to 31, all different within a row; in each aligned block of 4 rows (0 to 3, 4 to 7, ...) at most 2 rows name the same one
- gate_values: float32 [1024, 8], P(('ctx', 'exp')), may hold values from 0.05 to 1
- w_gate_up: bfloat16 [32, 4096, 3072], P('exp', 'ctx'), may hold values from -0.09375 to 0.09375
- w_down: bfloat16 [32, 1536, 4096], P('exp', None, 'ctx'), may hold values from -0.15625 to 0.15625
Outputs:
- layer_out: float32 [1024, 4096], P(('ctx', 'exp'))
- head_max: float32 [64], P('exp')
Inputs may be any that keep to these rules, and one draw needn't show every extreme that they name: `expert_ids`: each row names 8 different experts; in the rows of one device no expert is named more than 2 times.
All inputs are finite; a program needn't handle non-finite values.
Results may differ from a plain program's by a relative error of at most 0.018.
Values may be sent and summed in bfloat16 or wider, within the bound.
A program may use at most 192 MiB of HBM per device.

v0:
```python
import math
import jax
import jax.numpy as jnp
from jax import lax
from jax.sharding import PartitionSpec as P

D = 4096
HEADS = 64
KVH = 4
HD = 128
FF = 1536
TOP = 8
EXPERTS = 32
eps = 1e-06


def attend_block(carry_state, q_rows, k_block, v_block, q_pos):
    weighted, row_peak, row_total = carry_state
    score_scale = 1.0 / math.sqrt(q_rows.shape[1])
    scores = (
        jnp.einsum("rd,kd->rk", q_rows, k_block, preferred_element_type=jnp.float32) * score_scale
    )
    k_pos = jnp.arange(k_block.shape[0], dtype=jnp.int32)
    visible = k_pos[None, :] <= q_pos[:, None]
    masked = jnp.where(visible, scores, -1e30)
    new_peak = jnp.maximum(row_peak, jnp.max(masked, axis=1))
    weights = jnp.where(visible, jnp.exp(masked - new_peak[:, None]), 0.0)
    row_total = jnp.sum(weights, axis=1)
    weighted = jnp.dot(weights.astype(jnp.bfloat16), v_block, preferred_element_type=jnp.float32)
    return (weighted, new_peak, row_total)


def local(
    query, keys, values, out_weight, residual, norm_gain, expert_ids, gate_values, w_gate_up, w_down
):
    ctx_count = lax.axis_size("ctx")
    exp_count = lax.axis_size("exp")
    ctx_index = lax.axis_index("ctx")
    exp_index = lax.axis_index("exp")
    q_local, q_width = query.shape
    head_count = q_width // HD
    key_local = keys.shape[0]
    length = key_local * ctx_count
    slab_rows = q_local * ctx_count
    kv_index = exp_index * head_count // (HEADS // KVH)
    k_head = lax.dynamic_slice_in_dim(keys, kv_index * HD, HD, 1)
    v_head = lax.dynamic_slice_in_dim(values, kv_index * HD, HD, 1)
    q_rows = (
        query.reshape(q_local, head_count, HD).transpose(1, 0, 2).reshape(head_count * q_local, HD)
    )
    row_offsets = jnp.tile(jnp.arange(q_local, dtype=jnp.int32), head_count)
    flat_rows = head_count * q_local
    start_state = (
        jnp.zeros((flat_rows, HD), jnp.float32),
        jnp.full((flat_rows,), -1e30, jnp.float32),
        jnp.zeros((flat_rows,), jnp.float32),
    )
    q_pos = length - slab_rows + ctx_index * q_local + row_offsets
    weighted, row_peak, row_total = attend_block(
        start_state,
        q_rows,
        lax.all_gather(k_head, "ctx", axis=0, tiled=True),
        lax.all_gather(v_head, "ctx", axis=0, tiled=True),
        q_pos,
    )
    attended = (weighted / row_total[:, None]).astype(jnp.bfloat16)
    attended = (
        attended.reshape(head_count, q_local, HD)
        .transpose(1, 0, 2)
        .reshape(q_local, head_count * HD)
    )
    head_peak = jnp.max(row_peak.reshape(head_count, q_local), axis=1)
    head_max = lax.pmax(head_peak, "ctx")
    part_rows = attended
    projected = lax.psum_scatter(
        jnp.dot(part_rows, out_weight, preferred_element_type=jnp.float32),
        "exp",
        scatter_dimension=0,
        tiled=True,
    )
    state_rows = residual.astype(jnp.float32) + projected
    normed = (
        state_rows
        * lax.rsqrt(jnp.mean(state_rows * state_rows, axis=1, keepdims=True) + eps)
        * norm_gain
    ).astype(jnp.bfloat16)
    local_rows = normed.shape[0]
    slot_cap = max(2, 2 * local_rows * TOP // EXPERTS)
    slot_count = slot_cap * EXPERTS
    flat_ids = expert_ids.reshape(-1)
    onehot_ids = (flat_ids[:, None] == jnp.arange(EXPERTS, dtype=jnp.int32)[None, :]).astype(
        jnp.int32
    )
    earlier = jnp.cumsum(onehot_ids, axis=0) - onehot_ids
    slot_rank = jnp.sum(earlier * onehot_ids, axis=1)
    target = slot_rank * EXPERTS + flat_ids
    slot_table = target[None, :] == jnp.arange(slot_count, dtype=jnp.int32)[:, None]
    place_rows = jnp.any(slot_table.reshape(slot_count, local_rows, TOP), axis=2).astype(
        jnp.bfloat16
    )
    outgoing = jnp.dot(place_rows, normed, preferred_element_type=jnp.float32).astype(jnp.bfloat16)
    outgoing = outgoing.reshape(1, 1, slot_cap, EXPERTS, D)
    incoming = lax.all_to_all(
        lax.all_to_all(outgoing, "ctx", split_axis=4, concat_axis=1, tiled=True),
        "exp",
        split_axis=3,
        concat_axis=0,
        tiled=True,
    )
    expert_local = w_down.shape[0]
    d_local = w_gate_up.shape[1]
    expert_rows = incoming.reshape(-1, expert_local, d_local)
    part_rows = expert_rows
    summed = lax.psum(
        jnp.einsum("mxd,xdf->mxf", part_rows, w_gate_up, preferred_element_type=jnp.float32).astype(
            jnp.bfloat16
        ),
        "ctx",
    ).astype(jnp.float32)
    inner_units = (jax.nn.silu(summed[..., :FF]) * summed[..., FF:]).astype(jnp.bfloat16)
    expert_out = jnp.einsum(
        "mxf,xfd->mxd", inner_units, w_down, preferred_element_type=jnp.float32
    ).astype(jnp.bfloat16)
    shaped = expert_out.reshape(exp_count, ctx_count, slot_cap, expert_local, d_local)
    returned = lax.all_to_all(
        lax.all_to_all(shaped, "ctx", split_axis=1, concat_axis=4, tiled=True),
        "exp",
        split_axis=0,
        concat_axis=3,
        tiled=True,
    )
    back_rows = returned.reshape(slot_count, D)
    pick_table = (target[:, None] == jnp.arange(slot_count, dtype=jnp.int32)[None, :]).astype(
        jnp.bfloat16
    )
    per_choice = jnp.dot(pick_table, back_rows, preferred_element_type=jnp.float32).reshape(
        local_rows, TOP, D
    )
    moe_sum = jnp.sum(per_choice * gate_values[:, :, None], axis=1)
    layer_out = state_rows + moe_sum
    return (layer_out, head_max)


def solution(mesh):
    return jax.shard_map(
        local,
        mesh=mesh,
        in_specs=(
            P("ctx", "exp"),
            P("ctx", None),
            P("ctx", None),
            P("exp", None),
            P(("ctx", "exp"), None),
            P(),
            P(("ctx", "exp"), None),
            P(("ctx", "exp"), None),
            P("exp", "ctx", None),
            P("exp", None, "ctx"),
        ),
        out_specs=(P(("ctx", "exp"), None), P("exp")),
        check_vma=False,
    )
```

profile of v0, /device:TPU:6, one launch (start us, length us, event | category | flops | bytes accessed | tf_op | source)
XLA Modules:
  0.0 649.4 jit_solution(4348917887009457203)
XLA Ops:
  7.2 2.0 constant_dynamic-slice_fusion.1
  9.3 1.9 constant_dynamic-slice_fusion
  12.3 77.6 %all-gather.3.cloned.1.call-done = bf16[32768,128]{1,0:T(8,128)(2,1)} async-done(((bf16[2048,128]{1,0:T(8,128)(2,1)}), bf16[32768,128]{1,0:T(8,128)(2,1)}) %all-gather.3.cloned.1.call-update) | async-done | bytes 8388624 | tf_op jit(solution)/shard_map/all_gather | solution.py:62
  89.8 19.2 %fusion.36 = (f32[256]{0:T(256)S(1)}, f32[256,32768]{0,1:T(8,128)}) fusion(bf16[32768,128]{1,0:T(8,128)(2,1)} %all-gather.3.cloned.1.call-done, bf16[256,128]{1,0:T(8,128)(2,1)S(1)} %bitcast.61, s32[256]{0:T(256)S(1)} %add.53), kind=kOutput, calls=%fused_computation.45 | convolution fusion | flops 2181037824 | bytes 42010624 | tf_op jit(solution)/shard_map/rd,kd->rk/dot_general | solution.py:21
  109.1 15.1 %fusion.2 = f32[256]{0:T(256)S(1)} fusion(f32[256,32768]{0,1:T(8,128)} %get-tuple-element.3, f32[256]{0:T(256)S(1)} %broadcast_maximum_fusion, s32[256]{0:T(256)S(1)} %add.53), kind=kLoop, calls=%fused_computation.5 | loop fusion | flops 33554176 | bytes 33557504 | tf_op jit(solution)/shard_map/reduce_sum | solution.py:28
  124.3 43.9 %all-gather.5.cloned.1.call-done = bf16[32768,128]{1,0:T(8,128)(2,1)} async-done(((bf16[2048,128]{1,0:T(8,128)(2,1)}), bf16[32768,128]{1,0:T(8,128)(2,1)}) %all-gather.5.cloned.1.call-update) | async-done | bytes 8388624 | tf_op jit(solution)/shard_map/all_gather | solution.py:63
  168.2 17.2 %fusion.19 = bf16[256,128]{1,0:T(8,128)(2,1)S(1)} fusion(bf16[32768,128]{1,0:T(8,128)(2,1)} %all-gather.5.cloned.1.call-done, f32[256,32768]{0,1:T(8,128)} %get-tuple-element.3, f32[256]{0:T(256)S(1)} %broadcast_maximum_fusion, s32[256]{0:T(256)S(1)} %add.53, f32[256]{0:T(256)S(1)} %fusion.2), kind=kOutput, calls=%fused_computation.18 | convolution fusion | flops 2181103616 | bytes 42011648 | tf_op jit(solution)/shard_map/dot_general | solution.py:29
  185.4 4.0 fusion.22
  191.6 137.2 %all-reduce.6.cloned.1.call-done = f32[64,4096]{1,0:T(8,128)} async-done(((f32[64,4096]{1,0:T(8,128)}), f32[64,4096]{1,0:T(8,128)}) %all-reduce.6.cloned.1.call-update) | async-done | bytes 1048592
  329.8 2.1 convolution_convert_fusion
  331.9 5.3 copy.33
  337.2 5.9 reshape.120
  343.1 16.8 %all_to_all.66 = bf16[16,2,8192]{2,1,0:T(2,128)(2,1)} all-to-all(bf16[16,2,8192]{2,1,0:T(2,128)(2,1)} %reshape.120), channel_id=1, replica_groups=mesh['ctx'=16,'exp'=16] {'ctx'}, dimensions={0} | all-to-all | bytes 1048576 | tf_op jit(solution)/shard_map/all_to_all | solution.py:104
  359.8 5.9 reshape.121
  365.7 4.1 copy.34
  369.9 23.2 %all_to_all.67 = bf16[1,16,2,32,256]{4,1,2,0,3:T(8,128)(2,1)S(1)} all-to-all(bf16[1,16,2,32,256]{4,1,2,0,3:T(8,128)(2,1)} %bitcast.56), channel_id=1, replica_groups=mesh['ctx'=16,'exp'=16] {'exp'}, dimensions={3} | all-to-all | bytes 1048576 | tf_op jit(solution)/shard_map/all_to_all | solution.py:103
  393.1 1.4 copy.36
  394.5 2.0 reshape.113
  396.5 5.5 convert_bitcast_fusion
  402.1 157.1 %all-reduce.4.cloned.1.call-done = bf16[512,2,3072]{2,0,1:T(8,128)(2,1)} async-done(((bf16[512,2,3072]{2,0,1:T(8,128)(2,1)}), bf16[512,2,3072]{2,0,1:T(8,128)(2,1)}) %all-reduce.4.cloned.1.call-update) | async-done | bytes 6291472 | tf_op jit(solution)/shard_map/psum | solution.py:114
  559.2 4.5 convert_element_type.46
  563.7 2.7 fusion.12
  566.4 2.1 reshape.114
  568.5 1.3 copy.37
  569.8 16.8 %all_to_all.68 = bf16[16,16,2,2,256]{4,0,3,2,1:T(8,128)(2,1)S(1)} all-to-all(bf16[16,16,2,2,256]{4,0,3,2,1:T(8,128)(2,1)S(1)} %copy.37), channel_id=1, replica_groups=mesh['ctx'=16,'exp'=16] {'ctx'}, dimensions={1} | all-to-all | bytes 1048576 | tf_op jit(solution)/shard_map/all_to_all | solution.py:126
  587.7 2.0 reshape.117
  589.7 8.5 %all-to-all-start.3 = ((bf16[16,1,2,2,4096]{4,3,2,1,0:T(2,128)(2,1)}), bf16[16,1,2,2,4096]{4,3,2,1,0:T(2,128)(2,1)}, u32[]{:S(2)}, u32[]{:S(2)}) async-start(bf16[16,1,2,2,4096]{4,3,2,1,0:T(2,128)(2,1)} %reshape.117), calls=%async_computation.3 | async-start | bytes 1048576 | tf_op jit(solution)/shard_map/all_to_all | solution.py:125
  598.4 37.2 %pmax.7 = f32[4]{0:T(128)} all-reduce(f32[4]{0:T(128)S(1)} %reduce_max.19), channel_id=1, replica_groups=mesh['ctx'=16,'exp'=16] {'ctx'}, use_global_device_ids=true, to_apply=%region_10.11 | all-reduce | flops 4 | bytes 32 | tf_op jit(solution)/shard_map/pmax | solution.py:73
  635.6 2.3 copy.40
  637.9 2.0 reshape.116
  639.9 1.4 fusion.15
  641.3 1.6 fusion.32
  (44 shorter events, 5.0 us)
Async XLA Ops:
  7.2 389.4 %copy-start = (bf16[2,256,3072]{2,1,0:T(8,128)(2,1)S(1)}, bf16[2,256,3072]{2,1,0:T(8,128)(2,1)}, u32[]{:S(2)}) copy-start(bf16[2,256,3072]{2,1,0:T(8,128)(2,1)} %param.18) | copy-start | bytes 9437188
  7.2 82.7 %all-gather.3.cloned.1.call-start = ((), (), s32[]{:S(2)}) async-start(), calls=%async_computation.4 | async-start | bytes 8912896 | tf_op jit(solution)/shard_map/all_gather | solution.py:62
  9.3 158.9 %all-gather.5.cloned.1.call-start = ((), (), s32[]{:S(2)}) async-start(), calls=%async_computation.5 | async-start | bytes 8912896 | tf_op jit(solution)/shard_map/all_gather | solution.py:63
  11.2 317.5 %all-reduce.6.cloned.1.call-start = ((), (), s32[]{:S(2)}) async-start(), calls=%async_computation.7 | async-start | bytes 2097152
  124.2 65.5 %copy-start.3 = (s32[4,8]{1,0:T(4,128)S(1)}, s32[4,8]{1,0:T(4,128)}, u32[]{:S(2)}) copy-start(s32[4,8]{1,0:T(4,128)} %param.16) | copy-start | bytes 388
  124.2 66.0 %copy-start.6 = (u32[256]{0:T(256)S(1)}, u32[256]{0:T(256)}, u32[]{:S(2)}) copy-start(u32[256]{0:T(256)} %constant.65) | copy-start | bytes 3076
  124.2 204.5 %copy-start.1 = (bf16[4,4096]{1,0:T(4,128)(2,1)S(1)}, bf16[4,4096]{1,0:T(4,128)(2,1)}, u32[]{:S(2)}) copy-start(bf16[4,4096]{1,0:T(4,128)(2,1)} %param.14) | copy-start | bytes 98308
  124.2 205.6 %copy-start.2 = (f32[4096]{0:T(1024)S(1)}, f32[4096]{0:T(1024)}, u32[]{:S(2)}) copy-start(f32[4096]{0:T(1024)} %param.15) | copy-start | bytes 49156
  189.5 369.7 %all-reduce.4.cloned.1.call-start = ((), (), s32[]{:S(2)}) async-start(), calls=%async_computation.6 | async-start | bytes 12582912 | tf_op jit(solution)/shard_map/psum | solution.py:114
  559.2 4.6 copy-start.5
  566.4 73.5 %copy-start.4 = (f32[4,8]{1,0:T(4,128)S(1)}, f32[4,8]{1,0:T(4,128)}, u32[]{:S(2)}) copy-start(f32[4,8]{1,0:T(4,128)} %param.17) | copy-start | bytes 388
  589.7 45.9 %all-to-all-start.3 = ((bf16[16,1,2,2,4096]{4,3,2,1,0:T(2,128)(2,1)}), bf16[16,1,2,2,4096]{4,3,2,1,0:T(2,128)(2,1)}, u32[]{:S(2)}, u32[]{:S(2)}) async-start(bf16[16,1,2,2,4096]{4,3,2,1,0:T(2,128)(2,1)} %reshape.117), calls=%async_computation.3 | async-start | bytes 1048576 | tf_op jit(solution)/shard_map/all_to_all | solution.py:125
Sparse Core Ops, SparseCore 0:
  10.7 79.0 all-gather.2
  92.6 75.5 all-gather.4
  189.6 139.0 all-reduce.5
  402.2 156.9 all-reduce.3
where the time goes:
time: 651 us; the launch traced here: 649 us
  waiting for transfers between devices  416 us (64%)
  blocking collectives  94 us (14%)
  matrix products  52.1 us (8%)
  local copies, waits for them, and re-layouts  41.2 us (6%)
  other arithmetic  22.8 us (4%)
  between operations  14.6 us (2%)
  starting transfers between devices  8.83 us (1%)
    psum x1, waiting for transfers between devices, local(): lax.psum(jnp.einsum('mxd,xdf->mxf', part_rows, w_gate_up, preferred_eleme...  157 us
    unnamed x5, waiting for transfers between devices  137 us
    all_gather x1, waiting for transfers between devices, local(): lax.all_gather(k_head, 'ctx', axis=0, tiled=True)  77.6 us
    all_gather x1, waiting for transfers between devices, local(): lax.all_gather(v_head, 'ctx', axis=0, tiled=True)  43.9 us
    pmax x1, blocking collectives, local(): head_max = lax.pmax(head_peak, 'ctx')  37.2 us
    all_to_all x1, blocking collectives, local(): lax.all_to_all(lax.all_to_all(outgoing, 'ctx', split_axis=4, concat_axis=...  23.2 us
    dot_general x1, matrix products, attend_block(): jnp.einsum('rd,kd->rk', q_rows, k_block, preferred_element_type=jnp.float32)  19.2 us
    dot_general x1, matrix products, attend_block(): jnp.dot(weights.astype(jnp.bfloat16), v_block, preferred_element_type=jnp...  17.2 us
  transfers between devices with their start and end apart: 5, of which 4 were waited for; matrix products, arithmetic and copies ran while one was open for 6% of the time, Pallas kernels for 0%

commit v1 on v0

--- a/solution.py
+++ b/solution.py
@@ -59,7 +59,9 @@
     weighted, row_peak, row_total = attend_block(
         start_state,
         q_rows,
-        lax.all_gather(k_head, "ctx", axis=0, tiled=True),
+        jnp.concatenate(
+            lax.all_to_all(jnp.stack([k_head] * lax.axis_size("ctx")), "ctx", 0, 0), axis=0
+        ),
         lax.all_gather(v_head, "ctx", axis=0, tiled=True),
         q_pos,
     )

time: 651 us -> 683 us (1.049)
  waiting for transfers between devices: 416 us -> 437 us
  starting transfers between devices: 8.83 us -> 16.4 us
    all_to_all x0 -> x1, waiting for transfers between devices: none -> 131 us  [local(): lax.all_to_all(jnp.stack([k_head] * lax.axis_size('ctx')), 'ctx', 0, 0)]
    all_gather x1 -> x0, waiting for transfers between devices: 77.6 us -> none  [local(): lax.all_gather(k_head, 'ctx', axis=0, tiled=True)]
    all_gather x1, waiting for transfers between devices: 43.9 us -> 0.02 us  [local(): lax.all_gather(v_head, 'ctx', axis=0, tiled=True)]
    unnamed x5 -> x4, waiting for transfers between devices: 137 us -> 149 us
    all_to_all x0 -> x1, starting transfers between devices: none -> 7.58 us  [local(): lax.all_to_all(jnp.stack([k_head] * lax.axis_size('ctx')), 'ctx', 0, 0)]
  transfers between devices with their start and end apart: 5 -> 5, of which waited for: 4 -> 3; matrix products, arithmetic and copies ran while one was open for 6% -> 6% of each run, Pallas kernels for 0% -> 0%
where the time goes in v1:
time: 683 us; the launch traced here: 681 us
  waiting for transfers between devices  437 us (64%)
  blocking collectives  94 us (14%)
  matrix products  51.9 us (8%)
  local copies, waits for them, and re-layouts  44.5 us (7%)
  other arithmetic  23 us (3%)
  starting transfers between devices  16.4 us (2%)
  between operations  14.6 us (2%)
    psum x1, waiting for transfers between devices, local(): lax.psum(jnp.einsum('mxd,xdf->mxf', part_rows, w_gate_up, preferred_eleme...  157 us
    unnamed x4, waiting for transfers between devices  149 us
    all_to_all x1, waiting for transfers between devices, local(): lax.all_to_all(jnp.stack([k_head] * lax.axis_size('ctx')), 'ctx', 0, 0)  131 us
    pmax x1, blocking collectives, local(): head_max = lax.pmax(head_peak, 'ctx')  37.2 us
    all_to_all x1, blocking collectives, local(): lax.all_to_all(lax.all_to_all(outgoing, 'ctx', split_axis=4, concat_axis=...  23.2 us
    dot_general x1, matrix products, attend_block(): jnp.einsum('rd,kd->rk', q_rows, k_block, preferred_element_type=jnp.float32)  19.1 us
    dot_general x1, matrix products, attend_block(): jnp.dot(weights.astype(jnp.bfloat16), v_block, preferred_element_type=jnp...  17.2 us
    all_to_all x1, blocking collectives, local(): lax.all_to_all(shaped, 'ctx', split_axis=1, concat_axis=4, tiled=True)  16.8 us
  transfers between devices with their start and end apart: 5, of which 3 were waited for; matrix products, arithmetic and copies ran while one was open for 6% of the time, Pallas kernels for 0%

profile of v1, /device:TPU:6, one launch (start us, length us, event | category | flops | bytes accessed | tf_op | source)
XLA Modules:
  0.0 681.4 jit_solution(3425378847347762580)
XLA Ops:
  7.2 2.0 constant_dynamic-slice_fusion
  10.4 4.8 stack.2
  15.2 7.6 %all-to-all-start = ((bf16[16,2048,128]{2,1,0:T(8,128)(2,1)}), bf16[16,2048,128]{2,1,0:T(8,128)(2,1)}, u32[]{:S(2)}, u32[]{:S(2)}) async-start(bf16[16,2048,128]{2,1,0:T(8,128)(2,1)} %stack.2), calls=%async_computation | async-start | bytes 16777216 | tf_op jit(solution)/shard_map/all_to_all | solution.py:63
  23.0 131.1 %all-to-all-done = bf16[16,2048,128]{2,1,0:T(8,128)(2,1)} async-done(((bf16[16,2048,128]{2,1,0:T(8,128)(2,1)}), bf16[16,2048,128]{2,1,0:T(8,128)(2,1)}, u32[]{:S(2)}, u32[]{:S(2)}) %all-to-all-start) | async-done | bytes 8388640 | tf_op jit(solution)/shard_map/all_to_all | solution.py:63
  154.1 19.1 %fusion.36 = (f32[256]{0:T(256)S(1)}, f32[256,32768]{0,1:T(8,128)}) fusion(bf16[32768,128]{1,0:T(8,128)(2,1)} %bitcast, bf16[256,128]{1,0:T(8,128)(2,1)S(1)} %bitcast.62, s32[256]{0:T(256)S(1)} %add.53), kind=kOutput, calls=%fused_computation.45 | convolution fusion | flops 2181037824 | bytes 42010624 | tf_op jit(solution)/shard_map/rd,kd->rk/dot_general | solution.py:21
  173.2 15.2 %fusion.2 = f32[256]{0:T(256)S(1)} fusion(f32[256,32768]{0,1:T(8,128)} %get-tuple-element.3, f32[256]{0:T(256)S(1)} %broadcast_maximum_fusion, s32[256]{0:T(256)S(1)} %add.53), kind=kLoop, calls=%fused_computation.5 | loop fusion | flops 33554176 | bytes 33557504 | tf_op jit(solution)/shard_map/reduce_sum | solution.py:28
  188.5 17.2 %fusion.19 = bf16[256,128]{1,0:T(8,128)(2,1)S(1)} fusion(bf16[32768,128]{1,0:T(8,128)(2,1)} %all-gather.2.cloned.1.call-done, f32[256,32768]{0,1:T(8,128)} %get-tuple-element.3, f32[256]{0:T(256)S(1)} %broadcast_maximum_fusion, s32[256]{0:T(256)S(1)} %add.53, f32[256]{0:T(256)S(1)} %fusion.2), kind=kOutput, calls=%fused_computation.18 | convolution fusion | flops 2181103616 | bytes 42011648 | tf_op jit(solution)/shard_map/dot_general | solution.py:29
  205.8 4.0 fusion.22
  211.9 148.9 %all-reduce.6.cloned.1.call-done = f32[64,4096]{1,0:T(8,128)} async-done(((f32[64,4096]{1,0:T(8,128)}), f32[64,4096]{1,0:T(8,128)}) %all-reduce.6.cloned.1.call-update) | async-done | bytes 1048592
  361.8 2.1 convolution_convert_fusion
  363.9 5.3 copy.33
  369.2 5.9 reshape.126
  375.1 16.8 %all_to_all.71 = bf16[16,2,8192]{2,1,0:T(2,128)(2,1)} all-to-all(bf16[16,2,8192]{2,1,0:T(2,128)(2,1)} %reshape.126), channel_id=1, replica_groups=mesh['ctx'=16,'exp'=16] {'ctx'}, dimensions={0} | all-to-all | bytes 1048576 | tf_op jit(solution)/shard_map/all_to_all | solution.py:106
  391.8 5.9 reshape.127
  397.7 4.1 copy.34
  401.9 23.2 %all_to_all.72 = bf16[1,16,2,32,256]{4,1,2,0,3:T(8,128)(2,1)S(1)} all-to-all(bf16[1,16,2,32,256]{4,1,2,0,3:T(8,128)(2,1)} %bitcast.57), channel_id=1, replica_groups=mesh['ctx'=16,'exp'=16] {'exp'}, dimensions={3} | all-to-all | bytes 1048576 | tf_op jit(solution)/shard_map/all_to_all | solution.py:105
  425.2 1.4 copy.36
  426.5 2.0 reshape.119
  428.6 5.5 convert_bitcast_fusion
  434.1 157.1 %all-reduce.4.cloned.1.call-done = bf16[512,2,3072]{2,0,1:T(8,128)(2,1)} async-done(((bf16[512,2,3072]{2,0,1:T(8,128)(2,1)}), bf16[512,2,3072]{2,0,1:T(8,128)(2,1)}) %all-reduce.4.cloned.1.call-update) | async-done | bytes 6291472 | tf_op jit(solution)/shard_map/psum | solution.py:116
  591.2 4.5 convert_element_type.46
  595.8 2.7 fusion.12
  598.4 2.1 reshape.120
  600.5 1.3 copy.37
  601.8 16.8 %all_to_all.73 = bf16[16,16,2,2,256]{4,0,3,2,1:T(8,128)(2,1)S(1)} all-to-all(bf16[16,16,2,2,256]{4,0,3,2,1:T(8,128)(2,1)S(1)} %copy.37), channel_id=1, replica_groups=mesh['ctx'=16,'exp'=16] {'ctx'}, dimensions={1} | all-to-all | bytes 1048576 | tf_op jit(solution)/shard_map/all_to_all | solution.py:128
  619.7 2.0 reshape.123
  621.7 8.5 %all-to-all-start.4 = ((bf16[16,1,2,2,4096]{4,3,2,1,0:T(2,128)(2,1)}), bf16[16,1,2,2,4096]{4,3,2,1,0:T(2,128)(2,1)}, u32[]{:S(2)}, u32[]{:S(2)}) async-start(bf16[16,1,2,2,4096]{4,3,2,1,0:T(2,128)(2,1)} %reshape.123), calls=%async_computation.4 | async-start | bytes 1048576 | tf_op jit(solution)/shard_map/all_to_all | solution.py:127
  630.4 37.2 %pmax.7 = f32[4]{0:T(128)} all-reduce(f32[4]{0:T(128)S(1)} %reduce_max.19), channel_id=1, replica_groups=mesh['ctx'=16,'exp'=16] {'ctx'}, use_global_device_ids=true, to_apply=%region_10.11 | all-reduce | flops 4 | bytes 32 | tf_op jit(solution)/shard_map/pmax | solution.py:75
  667.6 2.3 copy.40
  669.9 2.0 reshape.122
  671.9 1.4 fusion.15
  673.3 1.6 fusion.32
  (46 shorter events, 5.2 us)
Async XLA Ops:
  7.2 421.4 %copy-start = (bf16[2,256,3072]{2,1,0:T(8,128)(2,1)S(1)}, bf16[2,256,3072]{2,1,0:T(8,128)(2,1)}, u32[]{:S(2)}) copy-start(bf16[2,256,3072]{2,1,0:T(8,128)(2,1)} %param.18) | copy-start | bytes 9437188
  7.2 181.3 %all-gather.2.cloned.1.call-start = ((), (), s32[]{:S(2)}) async-start(), calls=%async_computation.5 | async-start | bytes 8912896 | tf_op jit(solution)/shard_map/all_gather | solution.py:65
  15.2 7.7 %copy-start.2 = (bf16[64,512]{1,0:T(8,128)(2,1)S(1)}, bf16[64,512]{1,0:T(8,128)(2,1)}, u32[]{:S(2)}) copy-start(bf16[64,512]{1,0:T(8,128)(2,1)} %param.10) | copy-start | bytes 196612
  15.2 138.9 %all-to-all-start = ((bf16[16,2048,128]{2,1,0:T(8,128)(2,1)}), bf16[16,2048,128]{2,1,0:T(8,128)(2,1)}, u32[]{:S(2)}, u32[]{:S(2)}) async-start(bf16[16,2048,128]{2,1,0:T(8,128)(2,1)} %stack.2), calls=%async_computation | async-start | bytes 16777216 | tf_op jit(solution)/shard_map/all_to_all | solution.py:63
  22.8 337.9 %all-reduce.6.cloned.1.call-start = ((), (), s32[]{:S(2)}) async-start(), calls=%async_computation.7 | async-start | bytes 2097152
  188.4 21.6 %copy-start.4 = (s32[4,8]{1,0:T(4,128)S(1)}, s32[4,8]{1,0:T(4,128)}, u32[]{:S(2)}) copy-start(s32[4,8]{1,0:T(4,128)} %param.16) | copy-start | bytes 388
  188.4 22.1 %copy-start.7 = (u32[256]{0:T(256)S(1)}, u32[256]{0:T(256)}, u32[]{:S(2)}) copy-start(u32[256]{0:T(256)} %constant.65) | copy-start | bytes 3076
  188.4 172.3 %copy-start.1 = (bf16[4,4096]{1,0:T(4,128)(2,1)S(1)}, bf16[4,4096]{1,0:T(4,128)(2,1)}, u32[]{:S(2)}) copy-start(bf16[4,4096]{1,0:T(4,128)(2,1)} %param.14) | copy-start | bytes 98308
  188.5 173.4 %copy-start.3 = (f32[4096]{0:T(1024)S(1)}, f32[4096]{0:T(1024)}, u32[]{:S(2)}) copy-start(f32[4096]{0:T(1024)} %param.15) | copy-start | bytes 49156
  209.8 381.4 %all-reduce.4.cloned.1.call-start = ((), (), s32[]{:S(2)}) async-start(), calls=%async_computation.6 | async-start | bytes 12582912 | tf_op jit(solution)/shard_map/psum | solution.py:116
  591.2 4.6 copy-start.6
  598.4 73.5 %copy-start.5 = (f32[4,8]{1,0:T(4,128)S(1)}, f32[4,8]{1,0:T(4,128)}, u32[]{:S(2)}) copy-start(f32[4,8]{1,0:T(4,128)} %param.17) | copy-start | bytes 388
  621.7 45.9 %all-to-all-start.4 = ((bf16[16,1,2,2,4096]{4,3,2,1,0:T(2,128)(2,1)}), bf16[16,1,2,2,4096]{4,3,2,1,0:T(2,128)(2,1)}, u32[]{:S(2)}, u32[]{:S(2)}) async-start(bf16[16,1,2,2,4096]{4,3,2,1,0:T(2,128)(2,1)} %reshape.123), calls=%async_computation.4 | async-start | bytes 1048576 | tf_op jit(solution)/shard_map/all_to_all | solution.py:127
Sparse Core Ops, SparseCore 0:
  10.7 165.5 all-gather.1
  209.9 150.7 all-reduce.5
  434.2 156.9 all-reduce.3
